TPU v7x, 32 devices: a whole 2x2x4 slice. The times are simulated.
32 devices in a mesh: occ: 16 (over z, y, x), blk: 2 (over core).
Axes of the slice: x: 2, y: 2, z: 4, core: 2. Of those that a mesh axis runs over, the one named last changes fastest.
Arguments:
- integrals: bfloat16 [20480, 16, 240], P(('occ', 'blk')), may hold values from -0.7 to 0.7
- domain_transforms: bfloat16 [32, 24, 24], replicated, may hold values from -1.25 to 1.25
- domain_lists: int32 [16, 2, 5], replicated, may hold values from 0 to 31, all different within a row
- occ_energies: float32 [16, 2, 1], P('occ'), may hold values from -1.5 to -0.4
- virt_energies: float32 [32, 24], replicated, may hold values from 0.3 to 2.5
- pair_pattern: int32 [16, 2, 2], P('occ'), may hold values from 0 to 1, as said below
Outputs:
- gradient_gamma: bfloat16 [20480, 16, 240], P(('occ', 'blk'))
Inputs may be any that keep to these rules, and one draw needn't show every extreme that they name: `domain_lists`: the 5 virtual blocks of each occupied block are distinct. `pair_pattern`: symmetric in its last two dimensions, with ones on the diagonal.
All inputs are finite; a program needn't handle non-finite values.
Results may differ from a plain program's by a relative error of at most 0.0049.
Values may be sent and summed in bfloat16 or wider, within the bound.
A program may use at most 128 MiB of HBM per device.

v0:
```python
import jax
import jax.numpy as jnp
from jax import lax
from jax.sharding import PartitionSpec as P

VB = 24
NDOM = 5
OB = 1


def build_fitted(raw_rows, transforms):
    row_count, group_count, width_all = raw_rows.shape
    block_count = transforms.shape[1]
    shaped = raw_rows.reshape(row_count, group_count, block_count, OB, NDOM, VB)
    mixed = jnp.einsum(
        "pgbomu,gbmuv->pgbomv", shaped, transforms, preferred_element_type=jnp.float32
    )
    return mixed.astype(jnp.bfloat16).reshape(row_count, group_count, width_all)


def on_device(
    integrals, domain_transforms, domain_lists, occ_energies, virt_energies, pair_pattern
):
    group_here = lax.axis_index("occ")
    own_lists = lax.dynamic_index_in_dim(domain_lists, group_here, 0, keepdims=True)
    every_transform = jnp.take(domain_transforms, domain_lists, axis=0)
    fitted_all = build_fitted(integrals, every_transform)
    fitted = lax.all_to_all(fitted_all, "occ", split_axis=1, concat_axis=0, tiled=True)
    aux_rows = fitted.shape[0]
    width_all = fitted.shape[2]
    fitted = fitted.reshape(aux_rows, width_all)
    block_count = pair_pattern.shape[1]
    width_block = width_all // block_count
    block_virt = jnp.take(virt_energies, own_lists[0], axis=0)
    col_energy = (occ_energies[0][:, :, None, None] - block_virt[:, None, :, :]).reshape(width_all)
    pattern_now = pair_pattern[0]
    pattern_float = pattern_now.astype(jnp.float32)
    mask_full = jnp.repeat(jnp.repeat(pattern_float, width_block, axis=0), width_block, axis=1)
    partial_sums = lax.dot_general(
        fitted, fitted, (((0,), (0,)), ((), ())), preferred_element_type=jnp.float32
    )
    row_sums = lax.psum_scatter(partial_sums, "blk", scatter_dimension=0, tiled=True)
    share_rows = row_sums.shape[0]
    block_here = lax.axis_index("blk")
    row_energy = lax.dynamic_slice_in_dim(col_energy, block_here * share_rows, share_rows, 0)
    row_mask = lax.dynamic_slice_in_dim(mask_full, block_here * share_rows, share_rows, 0)
    row_amplitudes = (row_mask * row_sums / (row_energy[:, None] + col_energy[None, :])).astype(
        jnp.bfloat16
    )
    amplitudes = lax.all_gather(row_amplitudes, "blk", axis=0, tiled=True)
    gamma_rows = lax.dot_general(
        fitted, amplitudes, (((1,), (1,)), ((), ())), preferred_element_type=jnp.float32
    )
    gamma_rows = gamma_rows.astype(jnp.bfloat16).reshape(aux_rows, 1, width_all)
    return lax.all_to_all(gamma_rows, "occ", split_axis=0, concat_axis=1, tiled=True)


def solution(mesh):
    return jax.shard_map(
        on_device,
        mesh=mesh,
        in_specs=(
            P(("occ", "blk"), None, None),
            P(),
            P(),
            P("occ", None, None),
            P(),
            P("occ", None, None),
        ),
        out_specs=P(("occ", "blk"), None, None),
        check_vma=False,
    )
```

profile of v0, /device:TPU:0, one launch (start us, length us, event | category | flops | bytes accessed | tf_op | source)
XLA Modules:
  0.0 350.3 jit_solution(12702951507838364540)
XLA Ops:
  6.5 0.7 compare_and_fusion
  7.2 0.7 compare_select_fusion
  7.9 0.1 copy.32
  8.1 0.1 copy.33
  8.2 0.1 reshape.104
  8.3 1.1 copy.34
  9.4 0.8 gather_fusion
  10.2 7.7 %convolution_convert_fusion.1 = bf16[16,2,5,24,640]{4,3,2,1,0:T(8,128)(2,1)} fusion(bf16[640,16,2,5,24]{0,4,3,2,1:T(8,128)(2,1)} %bitcast.50, bf16[16,2,5,24,24]{4,3,2,1,0:T(8,128)(2,1)S(1)} %bitcast.51, pred[16,2,5]{2,1,0:T(4,128)(4,1)S(1)} %copy.32), kind=kOutput, calls=%fused_computation.6 | convolution fusion | flops 120514560 | bytes 10014880 | tf_op jit(solution)/shard_map/pgbomu,gbmuv->pgbomv/dot_general | solution.py:15
  17.9 8.5 %all-to-all-start = ((bf16[640,16,240]{0,2,1:T(8,128)(2,1)}), bf16[640,16,240]{0,2,1:T(8,128)(2,1)}, u32[]{:S(2)}, u32[]{:S(2)}) async-start(bf16[640,16,240]{0,2,1:T(8,128)(2,1)} %bitcast.48), calls=%async_computation | async-start | bytes 9830400 | tf_op jit(solution)/shard_map/all_to_all | solution.py:28
  26.6 0.1 copy.37
  26.7 0.1 reshape.112
  26.8 92.5 %all-to-all-done = bf16[640,16,240]{0,2,1:T(8,128)(2,1)} async-done(((bf16[640,16,240]{0,2,1:T(8,128)(2,1)}), bf16[640,16,240]{0,2,1:T(8,128)(2,1)}, u32[]{:S(2)}, u32[]{:S(2)}) %all-to-all-start) | async-done | bytes 4915232 | tf_op jit(solution)/shard_map/all_to_all | solution.py:28
  119.3 6.0 %fusion.3 = f32[240,240]{1,0:T(8,128)} fusion(bf16[640,16,240]{0,2,1:T(8,128)(2,1)} %all-to-all-done), kind=kOutput, calls=%fused_computation.7 | convolution fusion | flops 1179648000 | bytes 5145600 | tf_op jit(solution)/shard_map/dot_general | solution.py:39
  125.5 0.1 broadcast_in_dim.38
  125.7 0.1 sub.21
  125.8 0.6 gather_fusion.1
  126.4 0.1 gather.12
  126.5 0.3 broadcast_in_dim.36
  126.8 0.2 reshape.99
  127.1 5.4 %copy.47 = bf16[30,8,16,640]{3,1,2,0:T(8,128)(2,1)} copy(bf16[30,8,16,640]{3,1,0,2:T(8,128)(2,1)} %bitcast.40) | data formatting | bytes 9830400
  132.5 18.3 %reduce-scatter.2.cloned.1.call-done = f32[120,240]{1,0:T(8,128)} async-done(((f32[240,240]{1,0:T(8,128)}), f32[120,240]{1,0:T(8,128)}) %reduce-scatter.2.cloned.1.call-update) | async-done | bytes 115216 | tf_op jit(solution)/shard_map/reduce_scatter | solution.py:42
  150.8 1.0 divide_convert_fusion
  151.8 1.9 all_gather.3
  153.7 6.0 %fusion = bf16[10240,1,240]{0,2,1:T(8,128)(2,1)} fusion(bf16[240,240]{1,0:T(8,128)(2,1)S(1)} %all_gather.3, bf16[10240,240]{0,1:T(8,128)(2,1)} %bitcast.49), kind=kOutput, calls=%fused_computation.3 | convolution fusion | flops 1182105600 | bytes 9945600 | tf_op jit(solution)/shard_map/dot_general | solution.py:51
  159.7 0.5 broadcast.60
  160.2 7.5 %reduce = bf16[10240,240]{0,1:T(8,128)(2,1)} reduce(bf16[10240,1,240]{0,2,1:T(8,128)(2,1)} %fusion, bf16[]{:T(256)} %broadcast.60), dimensions={1}, to_apply=%copy.40.reduce_sub_computation | reduce | bytes 9830402 | tf_op jit(solution)/shard_map/reshape | solution.py:54
  167.7 7.8 %copy.49 = bf16[10240,240]{1,0:T(8,128)(2,1)} copy(bf16[10240,240]{0,1:T(8,128)(2,1)} %reduce) | data formatting | bytes 9830400
  175.6 15.3 %reshape.124 = bf16[16,2,76800]{2,1,0:T(2,128)(2,1)} reshape(bf16[10240,240]{1,0:T(8,128)(2,1)} %copy.49) | data formatting | bytes 9830400
  190.9 117.2 %all_to_all.33 = bf16[16,2,76800]{2,1,0:T(2,128)(2,1)} all-to-all(bf16[16,2,76800]{2,1,0:T(2,128)(2,1)} %reshape.124), channel_id=1, replica_groups=mesh['occ'=16,'blk'=2] {'occ'}, dimensions={0} | all-to-all | bytes 9830400 | tf_op jit(solution)/shard_map/all_to_all | solution.py:55
  308.1 19.6 %reshape.125 = bf16[10240,1,240]{2,1,0:T(2,128)(2,1)} reshape(bf16[16,2,76800]{2,1,0:T(2,128)(2,1)} %all_to_all.33) | data formatting | bytes 9830400
  327.7 8.0 %copy.46 = bf16[10240,1,240]{2,0,1:T(8,128)(2,1)} copy(bf16[10240,1,240]{2,1,0:T(2,128)(2,1)} %reshape.125) | data formatting | bytes 9830400
  335.8 7.7 %copy.42 = bf16[640,16,240]{0,2,1:T(8,128)(2,1)} copy(bf16[640,16,240]{2,0,1:T(8,128)(2,1)} %bitcast.47) | data formatting | bytes 9830400 | tf_op jit(solution)/shard_map/all_to_all | solution.py:55
  (22 shorter events, 0.5 us)
Async XLA Ops:
  17.9 8.6 %copy-start = (s32[16,2,5]{0,1,2:T(2,128)S(1)}, s32[16,2,5]{0,1,2:T(2,128)}, u32[]{:S(2)}) copy-start(s32[16,2,5]{0,1,2:T(2,128)} %param.8) | copy-start | bytes 1924
  17.9 101.4 %all-to-all-start = ((bf16[640,16,240]{0,2,1:T(8,128)(2,1)}), bf16[640,16,240]{0,2,1:T(8,128)(2,1)}, u32[]{:S(2)}, u32[]{:S(2)}) async-start(bf16[640,16,240]{0,2,1:T(8,128)(2,1)} %bitcast.48), calls=%async_computation | async-start | bytes 9830400 | tf_op jit(solution)/shard_map/all_to_all | solution.py:28
  26.4 124.4 %reduce-scatter.2.cloned.1.call-start = ((), (), s32[]{:S(2)}) async-start(), calls=%async_computation.3 | async-start | bytes 368640 | tf_op jit(solution)/shard_map/reduce_scatter | solution.py:42
  26.8 98.8 %copy-start.3 = (f32[1,2,1]{1,2,0:T(1,128)S(1)}, f32[1,2,1]{1,2,0:T(1,128)}, u32[]{:S(2)}) copy-start(f32[1,2,1]{1,2,0:T(1,128)} %param.9) | copy-start | bytes 28
  26.8 99.0 %copy-start.1 = (f32[32,24]{0,1:T(8,128)S(1)}, f32[32,24]{0,1:T(8,128)}, u32[]{:S(2)}) copy-start(f32[32,24]{0,1:T(8,128)} %param.10) | copy-start | bytes 9220
  26.8 99.7 %copy-start.2 = (s32[1,2,2]{2,1,0:T(2,128)S(1)}, s32[1,2,2]{2,1,0:T(2,128)}, u32[]{:S(2)}) copy-start(s32[1,2,2]{2,1,0:T(2,128)} %param.11) | copy-start | bytes 52
Sparse Core Ops, SparseCore 0:
  125.5 25.2 reduce-scatter.1
where the time goes:
time: 352 us; the launch traced here: 350 us
  blocking collectives  119 us (34%)
  waiting for transfers between devices  111 us (32%)
  local copies, waits for them, and re-layouts  68.5 us (19%)
  matrix products  19.8 us (6%)
  between operations  13.5 us (4%)
  other arithmetic  9.92 us (3%)
  starting transfers between devices  8.56 us (2%)
    all_to_all x1, blocking collectives, on_device(): lax.all_to_all(gamma_rows, 'occ', split_axis=0, concat_axis=1, tiled=True)  117 us
    all_to_all x1, waiting for transfers between devices, on_device(): lax.all_to_all(fitted_all, 'occ', split_axis=1, concat_axis=0, tiled=True)  92.5 us
    unnamed x15, local copies, waits for them, and re-layouts  57.3 us
    reduce_scatter x1, waiting for transfers between devices, on_device(): lax.psum_scatter(partial_sums, 'blk', scatter_dimension=0, tiled=True)  18.3 us
    all_to_all x1, starting transfers between devices, on_device(): lax.all_to_all(fitted_all, 'occ', split_axis=1, concat_axis=0, tiled=True)  8.52 us
    dot_general x1, matrix products, build_fitted(): jnp.einsum('pgbomu,gbmuv->pgbomv', shaped, transforms, preferred_element_...  7.72 us
    all_to_all x1, local copies, waits for them, and re-layouts, on_device(): lax.all_to_all(gamma_rows, 'occ', split_axis=0, concat_axis=1, tiled=True)  7.71 us
    reshape x1, other arithmetic, on_device(): gamma_rows = gamma_rows.astype(jnp.bfloat16).reshape(aux_rows, 1, width_all)  7.5 us
  transfers between devices with their start and end apart: 2, of which 2 were waited for; matrix products, arithmetic and copies ran while one was open for 2% of the time, Pallas kernels for 0%

commit v1 on v0

--- a/solution.py
+++ b/solution.py
@@ -52,7 +52,10 @@
         fitted, amplitudes, (((1,), (1,)), ((), ())), preferred_element_type=jnp.float32
     )
     gamma_rows = gamma_rows.astype(jnp.bfloat16).reshape(aux_rows, 1, width_all)
-    return lax.all_to_all(gamma_rows, "occ", split_axis=0, concat_axis=1, tiled=True)
+    return jnp.concatenate(
+        lax.all_to_all(jnp.stack(jnp.split(gamma_rows, lax.axis_size("occ"), axis=0)), "occ", 0, 0),
+        axis=1,
+    )
 
 
 def solution(mesh):

time: 352 us -> 279 us (0.79)
  blocking collectives: 119 us -> 235 us
  waiting for transfers between devices: 111 us -> 0.02 us
  local copies, waits for them, and re-layouts: 68.5 us -> 15.4 us
  starting transfers between devices: 8.56 us -> 0.01 us
  matrix products: 19.8 us -> 11.5 us
  other arithmetic: 9.92 us -> 2.41 us
    all_to_all x1 -> x2, blocking collectives: 117 us -> 233 us  [the longest x1 118 us: on_device(): lax.all_to_all(fitted_all, 'occ', split_axis=1, concat_axis=0, tiled=True)]
    all_to_all x1 -> x0, waiting for transfers between devices: 92.5 us -> none  [on_device(): lax.all_to_all(fitted_all, 'occ', split_axis=1, concat_axis=0, tiled=True)]
    unnamed x15 -> x27, local copies, waits for them, and re-layouts: 57.3 us -> 11.7 us
    reduce_scatter x1, waiting for transfers between devices: 18.3 us -> 0.01 us  [on_device(): lax.psum_scatter(partial_sums, 'blk', scatter_dimension=0, tiled=True)]
    all_to_all x1 -> x0, starting transfers between devices: 8.52 us -> none  [on_device(): lax.all_to_all(fitted_all, 'occ', split_axis=1, concat_axis=0, tiled=True)]
    all_to_all x1 -> x0, local copies, waits for them, and re-layouts: 7.71 us -> none  [on_device(): lax.all_to_all(gamma_rows, 'occ', split_axis=0, concat_axis=1, tiled=True)]
    reshape x1 -> x0, other arithmetic: 7.5 us -> none  [on_device(): gamma_rows = gamma_rows.astype(jnp.bfloat16).reshape(aux_rows, 1, width_all)]
    dot_general x1, matrix products: 6.05 us -> 2.16 us  [on_device(): lax.dot_general(fitted, fitted, (((0,), (0,)), ((), ())), preferred_eleme...]
  transfers between devices with their start and end apart: 2 -> 1, of which waited for: 2 -> 0; matrix products, arithmetic and copies ran while one was open for 2% -> 3% of each run, Pallas kernels for 0% -> 0%
where the time goes in v1:
time: 279 us; the launch traced here: 278 us
  blocking collectives  235 us (84%)
  local copies, waits for them, and re-layouts  15.4 us (6%)
  between operations  13.6 us (5%)
  matrix products  11.5 us (4%)
    all_to_all x1, blocking collectives, on_device(): lax.all_to_all(fitted_all, 'occ', split_axis=1, concat_axis=0, tiled=True)  118 us
    all_to_all x1, blocking collectives, on_device(): lax.all_to_all(jnp.stack(jnp.split(gamma_rows, lax.axis_size('occ'), axis...  115 us
    unnamed x27, local copies, waits for them, and re-layouts  11.7 us
  transfers between devices with their start and end apart: 1, of which 0 were waited for; matrix products, arithmetic and copies ran while one was open for 3% of the time, Pallas kernels for 0%

profile of v1, /device:TPU:0, one launch (start us, length us, event | category | flops | bytes accessed | tf_op | source)
XLA Modules:
  0.0 278.1 jit_solution(6256943412401552125)
XLA Ops:
  6.5 0.7 compare_and_fusion
  7.2 0.7 compare_select_fusion
  7.9 0.8 constant_dynamic-slice_fusion
  8.7 0.1 copy.25
  8.8 0.1 reshape.149
  8.9 0.1 copy.20
  9.0 0.1 copy.21
  9.1 0.1 reshape.141
  9.2 1.1 copy.22
  10.3 0.8 gather_fusion
  11.2 5.5 %convolution_convert_fusion.1 = bf16[16,2,5,24,640]{4,3,2,1,0:T(8,128)(2,1)S(1)} fusion(bf16[640,16,2,5,24]{0,4,3,2,1:T(8,128)(2,1)} %bitcast.111, bf16[16,2,5,24,24]{4,3,2,1,0:T(8,128)(2,1)S(1)} %bitcast.112, pred[16,2,5]{2,1,0:T(4,128)(4,1)S(1)} %copy.20), kind=kOutput, calls=%fused_computation.5 | convolution fusion | flops 120514560 | bytes 10014880 | tf_op jit(solution)/shard_map/pgbomu,gbmuv->pgbomv/dot_general | solution.py:15
  16.6 118.0 %all_to_all.20 = bf16[640,16,240]{0,2,1:T(8,128)(2,1)S(1)} all-to-all(bf16[640,16,240]{0,2,1:T(8,128)(2,1)S(1)} %bitcast.109), channel_id=1, replica_groups=mesh['occ'=16,'blk'=2] {'occ'}, dimensions={1} | all-to-all | bytes 9830400 | tf_op jit(solution)/shard_map/all_to_all | solution.py:28
  134.7 2.2 copy-done
  136.9 2.2 fusion.2
  139.1 0.0 reduce-scatter.2.cloned.1.call-update
  139.1 0.1 broadcast_in_dim.37
  139.2 0.1 broadcast_in_dim.38
  139.3 0.0 copy-done.3
  139.3 0.1 sub.20
  139.4 0.1 sub.21
  139.5 0.1 copy.27
  139.5 0.6 gather_fusion.1
  140.1 0.1 gather.12
  140.2 0.3 broadcast_in_dim.36
  140.5 0.2 reshape.135
  140.7 0.1 dynamic_slice.12
  140.8 5.4 %copy.29 = bf16[30,8,16,640]{3,1,2,0:T(8,128)(2,1)} copy(bf16[30,8,16,640]{3,1,0,2:T(8,128)(2,1)} %bitcast.108) | data formatting | bytes 9830400
  146.2 1.0 divide_convert_fusion
  147.2 1.9 all_gather.3
  149.1 3.8 %convolution_convert_fusion = bf16[10240,240]{0,1:T(8,128)(2,1)S(1)} fusion(bf16[240,240]{1,0:T(8,128)(2,1)S(1)} %all_gather.3, bf16[10240,240]{0,1:T(8,128)(2,1)} %bitcast.107), kind=kOutput, calls=%fused_computation.2 | convolution fusion | flops 1182105600 | bytes 9945600 | tf_op jit(solution)/shard_map/dot_general | solution.py:51
  153.7 115.3 %all_to_all.21 = bf16[16,640,1,240]{1,3,2,0:T(8,128)(2,1)S(1)} all-to-all(bf16[16,640,1,240]{1,3,2,0:T(8,128)(2,1)S(1)} %fusion.8), channel_id=1, replica_groups=mesh['occ'=16,'blk'=2] {'occ'}, dimensions={0} | all-to-all | bytes 9830400 | tf_op jit(solution)/shard_map/all_to_all | solution.py:56
  269.0 2.3 copy.47
  (30 shorter events, 0.7 us)
Async XLA Ops:
  6.5 139.7 %reduce-scatter.2.cloned.1.call-start = ((), (), s32[]{:S(2)}) async-start(), calls=%async_computation.3 | async-start | bytes 368640 | tf_op jit(solution)/shard_map/reduce_scatter | solution.py:42
  134.7 2.3 copy-start
  136.9 2.4 copy-start.3
  136.9 2.5 copy-start.1
  136.9 3.3 %copy-start.2 = (s32[1,2,2]{2,1,0:T(2,128)S(1)}, s32[1,2,2]{2,1,0:T(2,128)}, u32[]{:S(2)}) copy-start(s32[1,2,2]{2,1,0:T(2,128)} %param.11) | copy-start | bytes 52
Sparse Core Ops, SparseCore 0:
  139.2 5.2 reduce-scatter.1
